TPU v7x, 32 devices: a whole 2x2x4 slice. The times are simulated.
32 devices in a mesh: cache: 8 (over z, x), owner: 4 (over y, core).
Axes of the slice: x: 2, y: 2, z: 4, core: 2. Of those that a mesh axis runs over, the one named last changes fastest.
Arguments:
- cache: bfloat16 [32, 4, 128, 256], P('cache'), may hold values from -2.5 to 2.5
- backing: bfloat16 [32, 32, 128, 256], P('cache', 'owner'), may hold values from -2.5 to 2.5
- resident: int32 [32, 4], P('cache'), may hold values from 0 to 31, as said below
- promote: int32 [32, 2], P('cache'), may hold values from 0 to 31, as said below
- victim: int32 [32, 2], P('cache'), may hold values from 0 to 3, as said below
- lookups: int32 [2, 4096, 32, 8], P(None, 'owner', 'cache'), may hold values from 0 to 511
- route: int32 [2, 4, 1024], P(None, 'owner'), may hold values from 0 to 1023, each once within a row
- dcn_down: bfloat16 [8192, 128], P('cache'), may hold values from -0.0625 to 0.0625
- dcn_up: bfloat16 [128, 8192], P(None, 'cache'), may hold values from -0.5 to 0.5
- dcn_bias: float32 [8192], replicated, may hold values from -5 to 5
- mlp_in: bfloat16 [8192, 1024], P('cache'), may hold values from -0.0625 to 0.0625
- mlp_bias: float32 [1024], replicated, may hold values from -3 to 3
- mlp_out: float32 [1024], replicated, may hold values from -0.1875 to 0.1875
- out_bias: float32 [1], replicated, may hold values from -4 to 4
Outputs:
- scores: float32 [2, 4, 1024], P(None, 'owner', 'cache')
- new_cache: bfloat16 [32, 4, 128, 256], P('cache')
- new_backing: bfloat16 [32, 32, 128, 256], P('cache', 'owner')
Inputs may be any that keep to these rules, and one draw needn't show every extreme that they name: `resident`: for each feature, 4 distinct backing blocks. `promote`: for each feature, 2 distinct backing blocks, none of them in that feature's resident; block k belongs to owner k // 8. `victim`: for each feature, 2 distinct slots. `route`: each batch and owner group holds every request index once.
All inputs are finite; a program needn't handle non-finite values.
Results may differ from a plain program's by a relative error of at most 0.004.
Values may be sent and summed in bfloat16 or wider, within the bound.
A program may use at most 128 MiB of HBM per device.

v0:
```python
import jax
import jax.numpy as jnp
from jax import lax
from jax.sharding import PartitionSpec as P


def take_rows(table, wanted):
    return jax.vmap(lambda rows, chosen: rows[chosen])(table, wanted)


def pool_batch(requests, order, table):
    requests = requests[order]
    count = requests.shape[0]
    step = min(512, count)
    codes = jnp.arange(table.shape[1], dtype=jnp.int32)

    def one_block(lookup_block):
        counts = jnp.sum((lookup_block[..., None] == codes).astype(jnp.bfloat16), axis=2)
        return jnp.einsum("rfk,fke->rfe", counts, table, preferred_element_type=jnp.float32).astype(
            jnp.bfloat16
        )

    blocks = requests.reshape((count // step, step) + requests.shape[1:])
    pooled = lax.map(one_block, blocks)
    return pooled.reshape((count,) + pooled.shape[2:])


def on_device(
    cache,
    backing,
    resident,
    promote,
    victim,
    lookups,
    route,
    dcn_down,
    dcn_up,
    dcn_bias,
    mlp_in,
    mlp_bias,
    mlp_out,
    out_bias,
):
    held = cache.shape[0]
    slots = cache.shape[1]
    block = cache.shape[2]
    width = cache.shape[3]
    own_blocks = backing.shape[1]
    promoted_count = promote.shape[1]
    owner_here = lax.axis_index("owner")
    local_index = promote - owner_here * own_blocks
    owned_here = (local_index >= 0) & (local_index < own_blocks)
    clamped = jnp.clip(local_index, 0, own_blocks - 1)
    fetched = take_rows(backing, clamped)
    outgoing = jnp.where(owned_here[:, :, None, None], fetched, jnp.zeros_like(fetched))
    arrived = lax.all_gather(outgoing, "owner", axis=0, tiled=True)
    owners = arrived.shape[0] // held
    arrived = arrived.reshape(owners, held, promoted_count, block, width)
    source = promote // own_blocks
    picked = source[None] == jnp.arange(owners, dtype=jnp.int32)[:, None, None]
    promoted = jnp.sum(jnp.where(picked[..., None, None], arrived, jnp.zeros_like(arrived)), axis=0)
    evicted = take_rows(cache, victim)
    leaving = take_rows(resident, victim) - owner_here * own_blocks
    slot_numbers = jnp.arange(slots, dtype=jnp.int32)
    block_numbers = jnp.arange(own_blocks, dtype=jnp.int32)
    new_cache = cache
    new_backing = backing
    for column in range(promoted_count):
        slot_hit = victim[:, column][:, None] == slot_numbers[None, :]
        new_cache = jnp.where(slot_hit[:, :, None, None], promoted[:, column][:, None], new_cache)
        block_hit = leaving[:, column][:, None] == block_numbers[None, :]
        new_backing = jnp.where(
            block_hit[:, :, None, None], evicted[:, column][:, None], new_backing
        )
    table = new_cache.reshape(held, slots * block, width)
    batches = lookups.shape[0]
    received = []
    for batch_turn in range(batches):
        pooled = pool_batch(lookups[batch_turn], route[batch_turn, 0], table)
        received.append(lax.all_to_all(pooled, "cache", split_axis=0, concat_axis=1, tiled=True))
    arrived_rows = jnp.stack(received)
    per_batch = arrived_rows.shape[1]
    features = arrived_rows.reshape(batches * per_batch, -1)
    low = jnp.dot(
        features,
        lax.all_gather(dcn_down, "cache", axis=0, tiled=True),
        preferred_element_type=jnp.float32,
    ).astype(jnp.bfloat16)
    gate = (
        jnp.dot(
            low,
            lax.all_gather(dcn_up, "cache", axis=1, tiled=True),
            preferred_element_type=jnp.float32,
        )
        + dcn_bias
    )
    crossed = (features * gate + features).astype(jnp.bfloat16)
    portion = mlp_in.shape[1] // lax.axis_size("owner")
    own_columns = lax.dynamic_slice_in_dim(mlp_in, owner_here * portion, portion, 1)
    column_block = lax.all_gather(own_columns, "cache", axis=0, tiled=True)
    before = jnp.dot(
        crossed,
        lax.all_gather(column_block, "owner", axis=1, tiled=True),
        preferred_element_type=jnp.float32,
    )
    hidden = jnp.maximum(before + mlp_bias, 0.0)
    scores = jnp.sum(hidden * mlp_out, axis=-1) + out_bias[0]
    return (scores.reshape(batches, 1, per_batch), new_cache, new_backing)


def solution(mesh):
    in_specs = (
        P("cache", None, None, None),
        P("cache", "owner", None, None),
        P("cache", None),
        P("cache", None),
        P("cache", None),
        P(None, "owner", "cache", None),
        P(None, "owner", None),
        P("cache", None),
        P(None, "cache"),
        P(),
        P("cache", None),
        P(),
        P(),
        P(),
    )
    out_specs = (
        P(None, "owner", "cache"),
        P("cache", None, None, None),
        P("cache", "owner", None, None),
    )
    return jax.shard_map(
        on_device, mesh=mesh, in_specs=in_specs, out_specs=out_specs, check_vma=False
    )
```

profile of v0, /device:TPU:0, one launch (start us, length us, event | category | flops | bytes accessed | tf_op | source)
XLA Modules:
  0.0 392.6 jit_solution(9065323531690684591)
XLA Ops:
  11.4 2.2 gather_fusion.2
  15.8 70.4 %all-gather.12.cloned.1.call-done = bf16[8192,256]{1,0:T(8,128)(2,1)} async-done(((bf16[1024,256]{1,0:T(8,128)(2,1)}), bf16[8192,256]{1,0:T(8,128)(2,1)}) %all-gather.12.cloned.1.call-update) | async-done | bytes 4194320 | tf_op jit(solution)/shard_map/all_gather | solution.py:100
  88.1 7.9 %gather_fusion = s32[1024,4,8]{2,1,0:T(4,128)} fusion(s32[1024,4,8]{2,1,0:T(4,128)S(1)} %bitcast.100, s32[1024]{0:T(1024)S(1)} %broadcast_clamp_fusion.1), kind=kCustom, calls=%fused_computation | custom fusion | bytes 266240 | tf_op jit(solution)/shard_map/gather | solution.py:12
  98.0 10.9 %all-gather.6.cloned.1.call-done = bf16[16,2,128,256]{3,2,1,0:T(8,128)(2,1)} async-done(((bf16[4,2,128,256]{3,2,1,0:T(8,128)(2,1)}), bf16[16,2,128,256]{3,2,1,0:T(8,128)(2,1)}) %all-gather.6.cloned.1.call-update) | async-done | bytes 2097168 | tf_op jit(solution)/shard_map/all_gather | solution.py:56
  108.9 2.1 select_reduce_fusion
  113.7 27.7 %while.26 = (s32[]{:T(128)}, bf16[2,512,4,256]{3,1,0,2:T(8,128)(2,1)}, s32[2,512,4,8]{1,3,2,0:T(8,128)S(1)}, bf16[4,512,256]{2,1,0:T(8,128)(2,1)}, s32[]{:T(128)}) while((s32[]{:T(128)}, bf16[2,512,4,256]{3,1,0,2:T(8,128)(2,1)}, s32[2,512,4,8]{1,3,2,0:T(8,128)S(1)}, bf16[4,512,256]{2,1,0:T(8,128)(2,1)}, s32[]{:T(128)}) %tuple.91), condition=%wide.region_3.4_spmd.clone, body=%wide.region_1.3_spmd.clone.sunk | while | flops 561512448 | bytes 10814045 | solution.py:24
  114.2 11.7 %fusion.60 = bf16[512,4,512]{2,1,0:T(4,128)(2,1)S(1)} fusion(s32[512,4,8]{2,1,0:T(4,128)S(1)} %copy.164), kind=kLoop, calls=%fused_computation.9.clone.1 | loop fusion | flops 24117248 | bytes 2162688 | tf_op jit(solution)/shard_map/while/body/eval_jaxpr/reduce_sum | solution.py:18
  128.0 11.7 %fusion.60 = bf16[512,4,512]{2,1,0:T(4,128)(2,1)S(1)} fusion(s32[512,4,8]{2,1,0:T(4,128)S(1)} %copy.164), kind=kLoop, calls=%fused_computation.9.clone.1 | loop fusion | flops 24117248 | bytes 2162688 | tf_op jit(solution)/shard_map/while/body/eval_jaxpr/reduce_sum | solution.py:18
  141.5 4.5 %copy.115 = bf16[1024,4,256]{2,1,0:T(4,128)(2,1)} copy(bf16[1024,4,256]{2,0,1:T(8,128)(2,1)} %bitcast.12) | data formatting | bytes 4194304 | tf_op jit(solution)/shard_map/reshape | solution.py:25
  146.0 5.5 %all-to-all-start = ((bf16[1024,4,256]{2,1,0:T(4,128)(2,1)}), bf16[1024,4,256]{2,1,0:T(4,128)(2,1)}, u32[]{:S(2)}, u32[]{:S(2)}) async-start(bf16[1024,4,256]{2,1,0:T(4,128)(2,1)} %copy.115), calls=%async_computation | async-start | bytes 4194304 | tf_op jit(solution)/shard_map/all_to_all | solution.py:80
  152.3 7.9 %gather_fusion.1 = s32[1024,4,8]{2,1,0:T(4,128)} fusion(s32[1024,4,8]{2,1,0:T(4,128)S(1)} %bitcast.101, s32[1024]{0:T(1024)S(1)} %broadcast_clamp_fusion), kind=kCustom, calls=%fused_computation.1 | custom fusion | bytes 266240 | tf_op jit(solution)/shard_map/gather | solution.py:12
  163.6 27.7 %while.27 = (s32[]{:T(128)}, bf16[2,512,4,256]{3,1,0,2:T(8,128)(2,1)}, s32[2,512,4,8]{1,3,2,0:T(8,128)S(1)}, bf16[4,512,256]{2,1,0:T(8,128)(2,1)}, s32[]{:T(128)}) while((s32[]{:T(128)}, bf16[2,512,4,256]{3,1,0,2:T(8,128)(2,1)}, s32[2,512,4,8]{1,3,2,0:T(8,128)S(1)}, bf16[4,512,256]{2,1,0:T(8,128)(2,1)}, s32[]{:T(128)}) %tuple.92), condition=%wide.region_6.7_spmd.clone, body=%wide.region_4.6_spmd.clone.sunk | while | flops 561512448 | bytes 10814045 | solution.py:24
  164.0 11.7 %fusion.64 = bf16[512,4,512]{2,1,0:T(4,128)(2,1)S(1)} fusion(s32[512,4,8]{2,1,0:T(4,128)S(1)} %copy.166), kind=kLoop, calls=%fused_computation.18.clone.1 | loop fusion | flops 24117248 | bytes 2162688 | tf_op jit(solution)/shard_map/while/body/eval_jaxpr/reduce_sum | solution.py:18
  177.9 11.7 %fusion.64 = bf16[512,4,512]{2,1,0:T(4,128)(2,1)S(1)} fusion(s32[512,4,8]{2,1,0:T(4,128)S(1)} %copy.166), kind=kLoop, calls=%fused_computation.18.clone.1 | loop fusion | flops 24117248 | bytes 2162688 | tf_op jit(solution)/shard_map/while/body/eval_jaxpr/reduce_sum | solution.py:18
  191.3 4.6 %copy.122 = bf16[1024,4,256]{2,1,0:T(4,128)(2,1)} copy(bf16[1024,4,256]{2,0,1:T(8,128)(2,1)} %bitcast.20) | data formatting | bytes 4194304 | tf_op jit(solution)/shard_map/reshape | solution.py:25
  195.9 17.7 %all-to-all-done = bf16[1024,4,256]{2,1,0:T(4,128)(2,1)} async-done(((bf16[1024,4,256]{2,1,0:T(4,128)(2,1)}), bf16[1024,4,256]{2,1,0:T(4,128)(2,1)}, u32[]{:S(2)}, u32[]{:S(2)}) %all-to-all-start) | async-done | bytes 2097184 | tf_op jit(solution)/shard_map/all_to_all | solution.py:80
  213.6 4.6 %all-to-all-start.1 = ((bf16[1024,4,256]{2,1,0:T(4,128)(2,1)}), bf16[1024,4,256]{2,1,0:T(4,128)(2,1)}, u32[]{:S(2)}, u32[]{:S(2)}) async-start(bf16[1024,4,256]{2,1,0:T(4,128)(2,1)} %copy.122), calls=%async_computation.1 | async-start | bytes 4194304 | tf_op jit(solution)/shard_map/all_to_all | solution.py:80
  220.7 3.3 select_select_fusion
  227.4 53.9 %all-to-all-done.1 = bf16[1024,4,256]{2,1,0:T(4,128)(2,1)} async-done(((bf16[1024,4,256]{2,1,0:T(4,128)(2,1)}), bf16[1024,4,256]{2,1,0:T(4,128)(2,1)}, u32[]{:S(2)}, u32[]{:S(2)}) %all-to-all-start.1) | async-done | bytes 2097184 | tf_op jit(solution)/shard_map/all_to_all | solution.py:80
  285.3 2.4 copy.125
  287.7 6.3 %copy.142 = bf16[32,8,32,256]{3,1,2,0:T(8,128)(2,1)} copy(bf16[32,8,32,256]{3,2,1,0:T(8,128)(2,1)S(1)} %bitcast.99) | data formatting | bytes 8388608
  294.0 4.3 %convolution_convert_fusion = bf16[256,128]{1,0:T(8,128)(2,1)S(1)} fusion(bf16[256,8192]{1,0:T(8,128)(2,1)} %bitcast.97, bf16[8192,128]{1,0:T(8,128)(2,1)} %all-gather.8.cloned.1.call-done), kind=kOutput, calls=%fused_computation.35 | convolution fusion | flops 536903680 | bytes 6356992 | tf_op jit(solution)/shard_map/dot_general | solution.py:84
  298.3 74.4 %all-gather.14.cloned.1.call-done = bf16[8192,1024]{1,0:T(8,128)(2,1)} async-done(((bf16[8192,256]{1,0:T(8,128)(2,1)}), bf16[8192,1024]{1,0:T(8,128)(2,1)}) %all-gather.14.cloned.1.call-update) | async-done | bytes 16777232 | tf_op jit(solution)/shard_map/all_gather | solution.py:103
  372.7 12.8 %fusion.33 = f32[256]{0:T(256)S(1)} fusion(bf16[8192,1024]{1,0:T(8,128)(2,1)} %all-gather.14.cloned.1.call-done, bf16[256,128]{1,0:T(8,128)(2,1)S(1)} %convolution_convert_fusion, bf16[128,8192]{1,0:T(8,128)(2,1)} %all-gather.10.cloned.1.call-done, bf16[256,8192]{1,0:T(8,128)(2,1)} %bitcast.98, f32[8192]{0:T(1024)S(1)} %copy-done.12, ...), kind=kOutput, calls=%fused_computation.34 | convolution fusion | flops 4843372544 | bytes 23176192 | tf_op jit(solution)/shard_map/dot_general | solution.py:101
  (98 shorter events, 35.2 us)
Async XLA Ops:
  7.2 1.6 copy-start
  7.2 79.0 %all-gather.12.cloned.1.call-start = ((), (), s32[]{:S(2)}) async-start(), calls=%async_computation.5 | async-start | bytes 4718592 | tf_op jit(solution)/shard_map/all_gather | solution.py:100
  9.6 99.3 %all-gather.6.cloned.1.call-start = ((), (), s32[]{:S(2)}) async-start(), calls=%async_computation.2 | async-start | bytes 2621440 | tf_op jit(solution)/shard_map/all_gather | solution.py:56
  14.5 279.5 %all-gather.8.cloned.1.call-start = ((), (), s32[]{:S(2)}) async-start(), calls=%async_computation.3 | async-start | bytes 2359296 | tf_op jit(solution)/shard_map/all_gather | solution.py:86
  15.2 283.1 %all-gather.10.cloned.1.call-start = ((), (), s32[]{:S(2)}) async-start(), calls=%async_computation.4 | async-start | bytes 2359296 | tf_op jit(solution)/shard_map/all_gather | solution.py:92
  15.8 356.9 %all-gather.14.cloned.1.call-start = ((), (), s32[]{:S(2)}) async-start(), calls=%async_computation.6 | async-start | bytes 20971520 | tf_op jit(solution)/shard_map/all_gather | solution.py:103
  86.2 0.7 copy-start.9
  86.2 1.0 copy-start.8
  86.3 1.8 copy-start.10
  96.0 1.9 copy-start.11
  97.9 13.2 %copy-start.4 = (bf16[4,4,128,256]{3,2,1,0:T(8,128)(2,1)S(1)}, bf16[4,4,128,256]{3,2,1,0:T(8,128)(2,1)}, u32[]{:S(2)}) copy-start(bf16[4,4,128,256]{3,2,1,0:T(8,128)(2,1)} %param.18) | copy-start | bytes 3145732
  114.2 11.7 %copy-start.6 = (bf16[4,512,256]{2,1,0:T(8,128)(2,1)S(1)}, bf16[4,512,256]{2,1,0:T(8,128)(2,1)}, u32[]{:S(2)}) copy-start(bf16[4,512,256]{2,1,0:T(8,128)(2,1)} %get-tuple-element.305) | copy-start | bytes 3145732 | tf_op jit(solution)/shard_map/while
  128.0 11.7 %copy-start.6 = (bf16[4,512,256]{2,1,0:T(8,128)(2,1)S(1)}, bf16[4,512,256]{2,1,0:T(8,128)(2,1)}, u32[]{:S(2)}) copy-start(bf16[4,512,256]{2,1,0:T(8,128)(2,1)} %get-tuple-element.305) | copy-start | bytes 3145732 | tf_op jit(solution)/shard_map/while
  146.0 67.6 %all-to-all-start = ((bf16[1024,4,256]{2,1,0:T(4,128)(2,1)}), bf16[1024,4,256]{2,1,0:T(4,128)(2,1)}, u32[]{:S(2)}, u32[]{:S(2)}) async-start(bf16[1024,4,256]{2,1,0:T(4,128)(2,1)} %copy.115), calls=%async_computation | async-start | bytes 4194304 | tf_op jit(solution)/shard_map/all_to_all | solution.py:80
  164.0 11.7 %copy-start.7 = (bf16[4,512,256]{2,1,0:T(8,128)(2,1)S(1)}, bf16[4,512,256]{2,1,0:T(8,128)(2,1)}, u32[]{:S(2)}) copy-start(bf16[4,512,256]{2,1,0:T(8,128)(2,1)} %get-tuple-element.290) | copy-start | bytes 3145732 | tf_op jit(solution)/shard_map/while
  177.8 11.7 %copy-start.7 = (bf16[4,512,256]{2,1,0:T(8,128)(2,1)S(1)}, bf16[4,512,256]{2,1,0:T(8,128)(2,1)}, u32[]{:S(2)}) copy-start(bf16[4,512,256]{2,1,0:T(8,128)(2,1)} %get-tuple-element.290) | copy-start | bytes 3145732 | tf_op jit(solution)/shard_map/while
  195.9 23.1 %copy-start.5 = (bf16[4,4,128,256]{3,2,1,0:T(8,128)(2,1)S(1)}, bf16[4,4,128,256]{3,2,1,0:T(8,128)(2,1)}, u32[]{:S(2)}) copy-start(bf16[4,4,128,256]{3,2,1,0:T(8,128)(2,1)} %param.18) | copy-start | bytes 3145732
  195.9 23.7 %copy-start.2 = (s32[4,4]{1,0:T(4,128)S(1)}, s32[4,4]{1,0:T(4,128)}, u32[]{:S(2)}) copy-start(s32[4,4]{1,0:T(4,128)} %param.20) | copy-start | bytes 196
  213.6 67.7 %all-to-all-start.1 = ((bf16[1024,4,256]{2,1,0:T(4,128)(2,1)}), bf16[1024,4,256]{2,1,0:T(4,128)(2,1)}, u32[]{:S(2)}, u32[]{:S(2)}) async-start(bf16[1024,4,256]{2,1,0:T(4,128)(2,1)} %copy.122), calls=%async_computation.1 | async-start | bytes 4194304 | tf_op jit(solution)/shard_map/all_to_all | solution.py:80
  283.2 1.6 copy-start.3
  294.0 78.7 %copy-start.12 = (f32[8192]{0:T(1024)S(1)}, f32[8192]{0:T(1024)}, u32[]{:S(2)}) copy-start(f32[8192]{0:T(1024)} %param.27) | copy-start | bytes 98308
  294.0 78.7 %copy-start.13 = (f32[1024]{0:T(1024)S(1)}, f32[1024]{0:T(1024)}, u32[]{:S(2)}) copy-start(f32[1024]{0:T(1024)} %param.30) | copy-start | bytes 12292
  294.0 78.7 %copy-start.14 = (f32[1024]{0:T(1024)S(1)}, f32[1024]{0:T(1024)}, u32[]{:S(2)}) copy-start(f32[1024]{0:T(1024)} %param.29) | copy-start | bytes 12292
  372.7 13.3 %copy-start.1 = (bf16[1024,1024]{1,0:T(8,128)(2,1)S(1)}, bf16[1024,1024]{1,0:T(8,128)(2,1)}, u32[]{:S(2)}) copy-start(bf16[1024,1024]{1,0:T(8,128)(2,1)} %param.28) | copy-start | bytes 6291460
Sparse Core Ops, SparseCore 0:
  10.7 75.4 all-gather.11
  87.8 21.0 all-gather.5
  111.1 52.2 all-gather.7
  165.3 89.3 all-gather.9
  256.1 116.5 all-gather.13
where the time goes:
time: 393 us
  waiting for transfers between devices  229 us (58%)
  local copies, waits for them, and re-layouts  58.2 us (15%)
  other arithmetic  56.9 us (14%)
  matrix products  23.8 us (6%)
  between operations  14.7 us (4%)
  starting transfers between devices  10.3 us (3%)
    all_gather x1, waiting for transfers between devices, on_device(): lax.all_gather(column_block, 'owner', axis=1, tiled=True)  74.4 us
    all_to_all x2, waiting for transfers between devices, on_device(): lax.all_to_all(pooled, 'cache', split_axis=0, concat_axis=1, tiled=True)  71.6 us
    all_gather x1, waiting for transfers between devices, on_device(): column_block = lax.all_gather(own_columns, 'cache', axis=0, tiled=True)  70.4 us
    reduce_sum x4, other arithmetic, one_block(): jnp.sum((lookup_block[..., None] == codes).astype(jnp.bfloat16), axis=2)  46.9 us
    gather x2, local copies, waits for them, and re-layouts, pool_batch(): requests = requests[order]  15.9 us
    unnamed x31, local copies, waits for them, and re-layouts  15.5 us
    dot_general x1, matrix products, on_device(): jnp.dot(crossed, lax.all_gather(column_block, 'owner', axis=1, tiled=True...  12.8 us
    all_gather x1, waiting for transfers between devices, on_device(): arrived = lax.all_gather(outgoing, 'owner', axis=0, tiled=True)  10.9 us
  transfers between devices with their start and end apart: 7, of which 5 were waited for; matrix products, arithmetic and copies ran while one was open for 31% of the time, Pallas kernels for 0%

commit v1 on v0

--- a/solution.py
+++ b/solution.py
@@ -77,7 +77,14 @@
     received = []
     for batch_turn in range(batches):
         pooled = pool_batch(lookups[batch_turn], route[batch_turn, 0], table)
-        received.append(lax.all_to_all(pooled, "cache", split_axis=0, concat_axis=1, tiled=True))
+        received.append(
+            jnp.concatenate(
+                lax.all_to_all(
+                    jnp.stack(jnp.split(pooled, lax.axis_size("cache"), axis=0)), "cache", 0, 0
+                ),
+                axis=1,
+            )
+        )
     arrived_rows = jnp.stack(received)
     per_batch = arrived_rows.shape[1]
     features = arrived_rows.reshape(batches * per_batch, -1)

time: 393 us -> 364 us (0.926)
  waiting for transfers between devices: 229 us -> 186 us
  local copies, waits for them, and re-layouts: 58.2 us -> 69 us
    all_gather x1, waiting for transfers between devices: 74.4 us -> 41.3 us  [on_device(): lax.all_gather(column_block, 'owner', axis=1, tiled=True)]
    unnamed x31 -> x43, local copies, waits for them, and re-layouts: 15.5 us -> 37.6 us
    all_gather x1, waiting for transfers between devices: 10.9 us -> 0.3 us  [on_device(): arrived = lax.all_gather(outgoing, 'owner', axis=0, tiled=True)]
    reshape x2 -> x0, local copies, waits for them, and re-layouts: 9.14 us -> none  [pool_batch(): return pooled.reshape((count,) + pooled.shape[2:])]
    all_to_all x4 -> x0, local copies, waits for them, and re-layouts: 5.49 us -> none  [on_device(): lax.all_to_all(pooled, 'cache', split_axis=0, concat_axis=1, tiled=True)]
  transfers between devices with their start and end apart: 7 -> 7, of which waited for: 5 -> 5; matrix products, arithmetic and copies ran while one was open for 31% -> 37% of each run, Pallas kernels for 0% -> 0%
where the time goes in v1:
time: 364 us; the launch traced here: 363 us
  waiting for transfers between devices  186 us (51%)
  local copies, waits for them, and re-layouts  69 us (19%)
  other arithmetic  59.4 us (16%)
  matrix products  23.6 us (6%)
  between operations  14.6 us (4%)
  starting transfers between devices  10.2 us (3%)
    all_to_all x2, waiting for transfers between devices, on_device(): lax.all_to_all(jnp.stack(jnp.split(pooled, lax.axis_size('cache'), axis=0...  73 us
    all_gather x1, waiting for transfers between devices, on_device(): column_block = lax.all_gather(own_columns, 'cache', axis=0, tiled=True)  70.4 us
    reduce_sum x4, other arithmetic, one_block(): jnp.sum((lookup_block[..., None] == codes).astype(jnp.bfloat16), axis=2)  46.9 us
    all_gather x1, waiting for transfers between devices, on_device(): lax.all_gather(column_block, 'owner', axis=1, tiled=True)  41.3 us
    unnamed x43, local copies, waits for them, and re-layouts  37.6 us
    gather x2, local copies, waits for them, and re-layouts, pool_batch(): requests = requests[order]  15.9 us
    dot_general x1, matrix products, on_device(): jnp.dot(crossed, lax.all_gather(column_block, 'owner', axis=1, tiled=True...  12.7 us
    all_to_all x2, starting transfers between devices, on_device(): lax.all_to_all(jnp.stack(jnp.split(pooled, lax.axis_size('cache'), axis=0...  10 us
  transfers between devices with their start and end apart: 7, of which 5 were waited for; matrix products, arithmetic and copies ran while one was open for 37% of the time, Pallas kernels for 0%

profile of v1, /device:TPU:0, one launch (start us, length us, event | category | flops | bytes accessed | tf_op | source)
XLA Modules:
  0.0 363.3 jit_solution(2595879105080041692)
XLA Ops:
  11.4 2.2 gather_fusion.2
  15.8 70.4 %all-gather.12.cloned.1.call-done = bf16[8192,256]{1,0:T(8,128)(2,1)} async-done(((bf16[1024,256]{1,0:T(8,128)(2,1)}), bf16[8192,256]{1,0:T(8,128)(2,1)}) %all-gather.12.cloned.1.call-update) | async-done | bytes 4194320 | tf_op jit(solution)/shard_map/all_gather | solution.py:107
  88.1 7.9 %gather_fusion = s32[1024,4,8]{2,1,0:T(4,128)} fusion(s32[1024,4,8]{2,1,0:T(4,128)S(1)} %bitcast.162, s32[1024]{0:T(1024)S(1)} %get-tuple-element.216), kind=kCustom, calls=%fused_computation | custom fusion | bytes 266240 | tf_op jit(solution)/shard_map/gather | solution.py:12
  96.0 1.8 copy.89
  98.7 7.9 %gather_fusion.1 = s32[1024,4,8]{2,1,0:T(4,128)} fusion(s32[1024,4,8]{2,1,0:T(4,128)S(1)} %bitcast.163, s32[1024]{0:T(1024)S(1)} %get-tuple-element.215), kind=kCustom, calls=%fused_computation.1 | custom fusion | bytes 266240 | tf_op jit(solution)/shard_map/gather | solution.py:12
  106.6 1.9 copy.93
  108.9 2.1 select_reduce_fusion
  113.7 27.7 %while.26 = (s32[]{:T(128)}, bf16[2,512,4,256]{3,1,0,2:T(8,128)(2,1)}, s32[2,512,4,8]{1,3,2,0:T(8,128)S(1)}, bf16[4,512,256]{2,1,0:T(8,128)(2,1)}, s32[]{:T(128)}) while((s32[]{:T(128)}, bf16[2,512,4,256]{3,1,0,2:T(8,128)(2,1)}, s32[2,512,4,8]{1,3,2,0:T(8,128)S(1)}, bf16[4,512,256]{2,1,0:T(8,128)(2,1)}, s32[]{:T(128)}) %tuple.90), condition=%wide.region_3.4_spmd.clone, body=%wide.region_1.3_spmd.clone.sunk | while | flops 561512448 | bytes 10814045 | solution.py:24
  114.2 11.7 %fusion.76 = bf16[512,4,512]{2,1,0:T(4,128)(2,1)S(1)} fusion(s32[512,4,8]{2,1,0:T(4,128)S(1)} %copy.134), kind=kLoop, calls=%fused_computation.9.clone.1 | loop fusion | flops 24117248 | bytes 2162688 | tf_op jit(solution)/shard_map/while/body/eval_jaxpr/reduce_sum | solution.py:18
  128.0 11.7 %fusion.76 = bf16[512,4,512]{2,1,0:T(4,128)(2,1)S(1)} fusion(s32[512,4,8]{2,1,0:T(4,128)S(1)} %copy.134), kind=kLoop, calls=%fused_computation.9.clone.1 | loop fusion | flops 24117248 | bytes 2162688 | tf_op jit(solution)/shard_map/while/body/eval_jaxpr/reduce_sum | solution.py:18
  154.9 5.5 %all-to-all-start = ((bf16[8,128,4,256]{3,1,2,0:T(8,128)(2,1)}), bf16[8,128,4,256]{3,1,2,0:T(8,128)(2,1)}, u32[]{:S(2)}, u32[]{:S(2)}) async-start(bf16[8,128,4,256]{3,1,2,0:T(8,128)(2,1)} %fusion.42), calls=%async_computation | async-start | bytes 4194304 | tf_op jit(solution)/shard_map/all_to_all | solution.py:82
  161.9 27.7 %while.27 = (s32[]{:T(128)}, bf16[2,512,4,256]{3,1,0,2:T(8,128)(2,1)}, s32[2,512,4,8]{1,3,2,0:T(8,128)S(1)}, bf16[4,512,256]{2,1,0:T(8,128)(2,1)}, s32[]{:T(128)}) while((s32[]{:T(128)}, bf16[2,512,4,256]{3,1,0,2:T(8,128)(2,1)}, s32[2,512,4,8]{1,3,2,0:T(8,128)S(1)}, bf16[4,512,256]{2,1,0:T(8,128)(2,1)}, s32[]{:T(128)}) %tuple.91), condition=%wide.region_6.7_spmd.clone, body=%wide.region_4.6_spmd.clone.sunk | while | flops 561512448 | bytes 10814045 | solution.py:24
  162.3 11.7 %fusion.80 = bf16[512,4,512]{2,1,0:T(4,128)(2,1)S(1)} fusion(s32[512,4,8]{2,1,0:T(4,128)S(1)} %copy.136), kind=kLoop, calls=%fused_computation.18.clone.1 | loop fusion | flops 24117248 | bytes 2162688 | tf_op jit(solution)/shard_map/while/body/eval_jaxpr/reduce_sum | solution.py:18
  176.2 11.7 %fusion.80 = bf16[512,4,512]{2,1,0:T(4,128)(2,1)S(1)} fusion(s32[512,4,8]{2,1,0:T(4,128)S(1)} %copy.136), kind=kLoop, calls=%fused_computation.18.clone.1 | loop fusion | flops 24117248 | bytes 2162688 | tf_op jit(solution)/shard_map/while/body/eval_jaxpr/reduce_sum | solution.py:18
  203.0 31.5 %all-to-all-done = bf16[8,128,4,256]{3,1,2,0:T(8,128)(2,1)} async-done(((bf16[8,128,4,256]{3,1,2,0:T(8,128)(2,1)}), bf16[8,128,4,256]{3,1,2,0:T(8,128)(2,1)}, u32[]{:S(2)}, u32[]{:S(2)}) %all-to-all-start) | async-done | bytes 2097184 | tf_op jit(solution)/shard_map/all_to_all | solution.py:82
  234.5 4.5 %all-to-all-start.1 = ((bf16[8,128,4,256]{3,1,2,0:T(8,128)(2,1)}), bf16[8,128,4,256]{3,1,2,0:T(8,128)(2,1)}, u32[]{:S(2)}, u32[]{:S(2)}) async-start(bf16[8,128,4,256]{3,1,2,0:T(8,128)(2,1)} %fusion.34), calls=%async_computation.1 | async-start | bytes 4194304 | tf_op jit(solution)/shard_map/all_to_all | solution.py:82
  241.5 3.6 select_select_fusion
  245.1 41.6 %all-to-all-done.1 = bf16[8,128,4,256]{3,1,2,0:T(8,128)(2,1)} async-done(((bf16[8,128,4,256]{3,1,2,0:T(8,128)(2,1)}), bf16[8,128,4,256]{3,1,2,0:T(8,128)(2,1)}, u32[]{:S(2)}, u32[]{:S(2)}) %all-to-all-start.1) | async-done | bytes 2097184 | tf_op jit(solution)/shard_map/all_to_all | solution.py:82
  286.7 2.6 pad_maximum_fusion
  289.3 2.4 copy.95
  291.7 6.3 %copy.112 = bf16[32,8,32,256]{3,1,2,0:T(8,128)(2,1)} copy(bf16[32,8,32,256]{3,2,1,0:T(8,128)(2,1)S(1)} %bitcast.161) | data formatting | bytes 8388608
  298.0 4.1 %convolution_convert_fusion = bf16[256,128]{1,0:T(8,128)(2,1)S(1)} fusion(bf16[256,8192]{1,0:T(8,128)(2,1)} %bitcast.159, bf16[8192,128]{1,0:T(8,128)(2,1)} %all-gather.8.cloned.1.call-done), kind=kOutput, calls=%fused_computation.35 | convolution fusion | flops 536903680 | bytes 6356992 | tf_op jit(solution)/shard_map/dot_general | solution.py:91
  302.2 41.3 %all-gather.14.cloned.1.call-done = bf16[8192,1024]{1,0:T(8,128)(2,1)} async-done(((bf16[8192,256]{1,0:T(8,128)(2,1)}), bf16[8192,1024]{1,0:T(8,128)(2,1)}) %all-gather.14.cloned.1.call-update) | async-done | bytes 16777232 | tf_op jit(solution)/shard_map/all_gather | solution.py:110
  343.5 12.7 %fusion.33 = f32[256]{0:T(256)S(1)} fusion(bf16[8192,1024]{1,0:T(8,128)(2,1)} %all-gather.14.cloned.1.call-done, bf16[256,128]{1,0:T(8,128)(2,1)S(1)} %convolution_convert_fusion, bf16[128,8192]{1,0:T(8,128)(2,1)} %all-gather.10.cloned.1.call-done, bf16[256,8192]{1,0:T(8,128)(2,1)} %bitcast.160, f32[8192]{0:T(1024)S(1)} %copy-done.11, ...), kind=kOutput, calls=%fused_computation.34 | convolution fusion | flops 4843372544 | bytes 23176192 | tf_op jit(solution)/shard_map/dot_general | solution.py:108
  (105 shorter events, 51.3 us)
Async XLA Ops:
  7.2 1.6 copy-start
  7.2 79.0 %all-gather.12.cloned.1.call-start = ((), (), s32[]{:S(2)}) async-start(), calls=%async_computation.5 | async-start | bytes 4718592 | tf_op jit(solution)/shard_map/all_gather | solution.py:107
  9.6 99.3 %all-gather.6.cloned.1.call-start = ((), (), s32[]{:S(2)}) async-start(), calls=%async_computation.2 | async-start | bytes 2621440 | tf_op jit(solution)/shard_map/all_gather | solution.py:56
  14.5 283.5 %all-gather.8.cloned.1.call-start = ((), (), s32[]{:S(2)}) async-start(), calls=%async_computation.3 | async-start | bytes 2359296 | tf_op jit(solution)/shard_map/all_gather | solution.py:93
  15.2 287.0 %all-gather.10.cloned.1.call-start = ((), (), s32[]{:S(2)}) async-start(), calls=%async_computation.4 | async-start | bytes 2359296 | tf_op jit(solution)/shard_map/all_gather | solution.py:99
  15.8 327.7 %all-gather.14.cloned.1.call-start = ((), (), s32[]{:S(2)}) async-start(), calls=%async_computation.6 | async-start | bytes 20971520 | tf_op jit(solution)/shard_map/all_gather | solution.py:110
  86.2 0.7 copy-start.8
  86.2 1.0 copy-start.7
  86.3 1.8 copy-start.9
  106.6 1.9 copy-start.10
  108.5 2.6 copy-start.3
  114.2 11.7 %copy-start.5 = (bf16[4,512,256]{2,1,0:T(8,128)(2,1)S(1)}, bf16[4,512,256]{2,1,0:T(8,128)(2,1)}, u32[]{:S(2)}) copy-start(bf16[4,512,256]{2,1,0:T(8,128)(2,1)} %get-tuple-element.299) | copy-start | bytes 3145732 | tf_op jit(solution)/shard_map/while
  128.0 11.7 %copy-start.5 = (bf16[4,512,256]{2,1,0:T(8,128)(2,1)S(1)}, bf16[4,512,256]{2,1,0:T(8,128)(2,1)}, u32[]{:S(2)}) copy-start(bf16[4,512,256]{2,1,0:T(8,128)(2,1)} %get-tuple-element.299) | copy-start | bytes 3145732 | tf_op jit(solution)/shard_map/while
  154.9 79.6 %all-to-all-start = ((bf16[8,128,4,256]{3,1,2,0:T(8,128)(2,1)}), bf16[8,128,4,256]{3,1,2,0:T(8,128)(2,1)}, u32[]{:S(2)}, u32[]{:S(2)}) async-start(bf16[8,128,4,256]{3,1,2,0:T(8,128)(2,1)} %fusion.42), calls=%async_computation | async-start | bytes 4194304 | tf_op jit(solution)/shard_map/all_to_all | solution.py:82
  162.3 11.7 %copy-start.6 = (bf16[4,512,256]{2,1,0:T(8,128)(2,1)S(1)}, bf16[4,512,256]{2,1,0:T(8,128)(2,1)}, u32[]{:S(2)}) copy-start(bf16[4,512,256]{2,1,0:T(8,128)(2,1)} %get-tuple-element.284) | copy-start | bytes 3145732 | tf_op jit(solution)/shard_map/while
  176.1 11.7 %copy-start.6 = (bf16[4,512,256]{2,1,0:T(8,128)(2,1)S(1)}, bf16[4,512,256]{2,1,0:T(8,128)(2,1)}, u32[]{:S(2)}) copy-start(bf16[4,512,256]{2,1,0:T(8,128)(2,1)} %get-tuple-element.284) | copy-start | bytes 3145732 | tf_op jit(solution)/shard_map/while
  203.0 36.9 %copy-start.4 = (bf16[4,4,128,256]{3,2,1,0:T(8,128)(2,1)S(1)}, bf16[4,4,128,256]{3,2,1,0:T(8,128)(2,1)}, u32[]{:S(2)}) copy-start(bf16[4,4,128,256]{3,2,1,0:T(8,128)(2,1)} %param.18) | copy-start | bytes 3145732
  203.0 37.5 %copy-start.2 = (s32[4,4]{1,0:T(4,128)S(1)}, s32[4,4]{1,0:T(4,128)}, u32[]{:S(2)}) copy-start(s32[4,4]{1,0:T(4,128)} %param.20) | copy-start | bytes 196
  234.5 52.2 %all-to-all-start.1 = ((bf16[8,128,4,256]{3,1,2,0:T(8,128)(2,1)}), bf16[8,128,4,256]{3,1,2,0:T(8,128)(2,1)}, u32[]{:S(2)}, u32[]{:S(2)}) async-start(bf16[8,128,4,256]{3,1,2,0:T(8,128)(2,1)} %fusion.34), calls=%async_computation.1 | async-start | bytes 4194304 | tf_op jit(solution)/shard_map/all_to_all | solution.py:82
  298.0 45.5 %copy-start.11 = (f32[8192]{0:T(1024)S(1)}, f32[8192]{0:T(1024)}, u32[]{:S(2)}) copy-start(f32[8192]{0:T(1024)} %param.27) | copy-start | bytes 98308
  298.0 45.5 %copy-start.12 = (f32[1024]{0:T(1024)S(1)}, f32[1024]{0:T(1024)}, u32[]{:S(2)}) copy-start(f32[1024]{0:T(1024)} %param.30) | copy-start | bytes 12292
  298.0 45.5 %copy-start.13 = (f32[1024]{0:T(1024)S(1)}, f32[1024]{0:T(1024)}, u32[]{:S(2)}) copy-start(f32[1024]{0:T(1024)} %param.29) | copy-start | bytes 12292
  343.5 13.3 %copy-start.1 = (bf16[1024,1024]{1,0:T(8,128)(2,1)S(1)}, bf16[1024,1024]{1,0:T(8,128)(2,1)}, u32[]{:S(2)}) copy-start(bf16[1024,1024]{1,0:T(8,128)(2,1)} %param.28) | copy-start | bytes 6291460
Sparse Core Ops, SparseCore 0:
  10.7 75.4 all-gather.11
  87.8 21.0 all-gather.5
  111.1 49.1 all-gather.7
  162.3 74.1 all-gather.9
  237.9 105.5 all-gather.13
